TPU v7x, 256 devices: a whole 4x4x8 slice. The times are simulated.
256 devices in a mesh: wide: 128 (over z, x, y), narrow: 2 (over core).
Axes of the slice: x: 4, y: 4, z: 8, core: 2. Of those that a mesh axis runs over, the one named last changes fastest.
Arguments:
- point_feats: bfloat16 [65536, 512], P(('wide', 'narrow')), may hold values from -24 to 24
- region_ids: int32 [16384], P(('wide', 'narrow')), may hold values from 0 to 63, as said below
- w_qkv: bfloat16 [512, 1536], replicated, may hold values from -0.25 to 0.25
- w_out: bfloat16 [512, 512], replicated, may hold values from -0.25 to 0.25
- w_expert_in: bfloat16 [512, 131072], P(None, 'wide'), may hold values from -0.25 to 0.25
- b_expert_in: float32 [131072], P('wide'), may hold values from -4 to 4
- w_expert_out: bfloat16 [131072, 512], P('wide'), may hold values from -0.125 to 0.125
- out_cotangent: bfloat16 [65536, 512], P(('wide', 'narrow')), may hold values from -18 to 18
Outputs:
- layer_out: bfloat16 [65536, 512], P(('wide', 'narrow'))
- grad_feats: bfloat16 [65536, 512], P(('wide', 'narrow'))
- grad_attention: float32 [512, 2048], P(('wide', 'narrow'))
- grad_expert_in: float32 [512, 131072], P('narrow', 'wide')
- grad_expert_out: float32 [131072, 512], P('wide', 'narrow')
- grad_expert_bias: float32 [131072], P(('wide', 'narrow'))
Inputs may be any that keep to these rules, and one draw needn't show every extreme that they name: `region_ids`: the 64 blocks of one device name any one region at most 2 times, and one region is named exactly 2 times by the blocks of every device.
All inputs are finite; a program needn't handle non-finite values.
Results may differ from a plain program's by a relative error of at most 0.0095.
Values may be sent and summed in bfloat16 or wider, within the bound.
No kernel may reach another device: no remote copies, remote signals or barrier semaphores. Data moves between devices by JAX's collectives and lax.ppermute only.
A program may use at most 128 MiB of HBM per device.

v0:
```python
import jax
import jax.numpy as jnp
from jax import lax
from jax.sharding import PartitionSpec as P

HEADS = 8
HID = 2048
DOMAIN_SPECIALS = 64
DOMAIN_REPEAT_CAP = 2


gelu_scale = 0.7978845608
gelu_cubic = 0.044715


def gelu_value(values):
    inner = gelu_scale * (values + gelu_cubic * values * values * values)
    return 0.5 * values * (1.0 + jnp.tanh(inner))


def gelu_slope(values):
    tangent = jnp.tanh(gelu_scale * (values + gelu_cubic * values * values * values))
    return 0.5 * (1.0 + tangent) + 0.5 * values * (1.0 - tangent * tangent) * gelu_scale * (
        1.0 + 3.0 * gelu_cubic * values * values
    )


def normalize_heads(raw):
    floats = raw.astype(jnp.float32)
    centred = floats - jnp.mean(floats, axis=-1, keepdims=True)
    scale_dev = jnp.sqrt(jnp.mean(centred * centred, axis=-1, keepdims=True) + 1e-05)
    normed = centred / scale_dev
    return (normed.astype(jnp.bfloat16), normed, scale_dev)


def normalize_back(grad_normed, normed, scale_dev):
    mean_grad = jnp.mean(grad_normed, axis=-1, keepdims=True)
    mean_cross = jnp.mean(grad_normed * normed, axis=-1, keepdims=True)
    return (grad_normed - mean_grad - normed * mean_cross) / scale_dev


def on_device(
    point_feats, region_ids, w_qkv, w_out, w_expert_in, b_expert_in, w_expert_out, out_cotangent
):
    wide_count = lax.axis_size("wide")
    narrow_count = lax.axis_size("narrow")
    points_local, width = point_feats.shape
    total_points = points_local * wide_count * narrow_count
    head_dim = width // HEADS
    qkv = jnp.dot(point_feats, w_qkv, preferred_element_type=jnp.float32).astype(jnp.bfloat16)
    queries = qkv[:, :width].reshape(points_local, HEADS, head_dim)
    key_norm, key_unit, key_scale = normalize_heads(
        qkv[:, width : 2 * width].reshape(points_local, HEADS, head_dim)
    )
    value_norm, value_unit, value_scale = normalize_heads(
        qkv[:, 2 * width :].reshape(points_local, HEADS, head_dim)
    )
    grad_mixed = jnp.einsum(
        "pc,ic->pi", out_cotangent, w_out, preferred_element_type=jnp.float32
    ).astype(jnp.bfloat16)
    grad_heads = grad_mixed.reshape(points_local, HEADS, head_dim)
    local_summary = jnp.einsum(
        "phi,phj->hij", key_norm, value_norm, preferred_element_type=jnp.float32
    )
    local_grad = jnp.einsum("phi,phj->hij", queries, grad_heads, preferred_element_type=jnp.float32)
    summary_total, grad_total = lax.psum((local_summary, local_grad), ("wide", "narrow"))
    summary_b = (summary_total / total_points).astype(jnp.bfloat16)
    grad_summary = grad_total / total_points
    mixed = (
        jnp.einsum("phi,hij->phj", queries, summary_b, preferred_element_type=jnp.float32)
        .astype(jnp.bfloat16)
        .reshape(points_local, width)
    )
    attention = jnp.dot(mixed, w_out, preferred_element_type=jnp.float32)
    grad_query = jnp.einsum(
        "phj,hij->phi", grad_heads, summary_b, preferred_element_type=jnp.float32
    ).astype(jnp.bfloat16)
    grad_keynorm = jnp.einsum("phj,hij->phi", value_norm.astype(jnp.float32), grad_summary)
    grad_valnorm = jnp.einsum("phi,hij->phj", key_norm.astype(jnp.float32), grad_summary)
    grad_key = normalize_back(grad_keynorm, key_unit, key_scale).astype(jnp.bfloat16)
    grad_value = normalize_back(grad_valnorm, value_unit, value_scale).astype(jnp.bfloat16)
    grad_qkv = jnp.concatenate(
        [
            grad_query.reshape(points_local, width),
            grad_key.reshape(points_local, width),
            grad_value.reshape(points_local, width),
        ],
        axis=1,
    )
    attention_back = jnp.einsum("pc,ic->pi", grad_qkv, w_qkv, preferred_element_type=jnp.float32)
    first_part = jnp.einsum("pi,pc->ic", point_feats, grad_qkv, preferred_element_type=jnp.float32)
    second_part = jnp.einsum("pi,pc->ic", mixed, out_cotangent, preferred_element_type=jnp.float32)
    grad_attention = lax.psum_scatter(
        jnp.concatenate([first_part, second_part], axis=1) / total_points,
        ("wide", "narrow"),
        scatter_dimension=0,
        tiled=True,
    )
    slab_cols = w_expert_in.shape[1]
    owner_count = max(1, wide_count // DOMAIN_SPECIALS)
    experts_here = max(1, DOMAIN_SPECIALS // wide_count)
    slot_cap = DOMAIN_REPEAT_CAP * experts_here
    blocks_local = region_ids.shape[0]
    block_len = points_local // blocks_local
    slot_total = wide_count * slot_cap
    dest_group = region_ids // experts_here
    same_group = dest_group[:, None] == dest_group[None, :]
    earlier = lax.broadcasted_iota(
        jnp.int32, (blocks_local, blocks_local), 1
    ) < lax.broadcasted_iota(jnp.int32, (blocks_local, blocks_local), 0)
    block_rank = jnp.sum((same_group & earlier).astype(jnp.int32), axis=1)
    first_dest = dest_group * owner_count
    slot_ids = jnp.arange(slot_total, dtype=jnp.int32)
    slot_dest = slot_ids // slot_cap
    slot_pos = slot_ids % slot_cap
    matches = (
        (slot_dest[:, None] >= first_dest[None, :])
        & (slot_dest[:, None] < first_dest[None, :] + owner_count)
        & (slot_pos[:, None] == block_rank[None, :])
    )
    filled = jnp.any(matches, axis=1)
    source_block = jnp.sum(
        jnp.where(matches, jnp.arange(blocks_local, dtype=jnp.int32)[None, :], 0), axis=1
    )
    send_labels = jnp.where(filled, region_ids[source_block], -1)

    def pack_rows(data):
        rows = jnp.take(data.reshape(blocks_local, block_len * width), source_block, axis=0)
        rows = jnp.where(filled[:, None], rows, jnp.zeros_like(rows))
        return rows.reshape(slot_total * block_len, width)

    col_expert = (
        lax.axis_index("wide") * slab_cols + jnp.arange(slab_cols, dtype=jnp.int32)
    ) // HID
    recv_feats, recv_labels = (
        lax.all_to_all(pack_rows(point_feats), "wide", split_axis=0, concat_axis=0, tiled=True),
        lax.all_to_all(send_labels, "wide", split_axis=0, concat_axis=0, tiled=True),
    )
    row_labels = jnp.repeat(recv_labels, block_len)
    live_mask = row_labels[:, None] == col_expert[None, :]
    pre_act = jnp.dot(recv_feats, w_expert_in, preferred_element_type=jnp.float32) + b_expert_in
    hidden = jnp.where(live_mask, gelu_value(pre_act), 0.0).astype(jnp.bfloat16)
    partial_out = jnp.dot(hidden, w_expert_out, preferred_element_type=jnp.float32).astype(
        jnp.bfloat16
    )
    live_mask, pre_act, hidden, partial_out = (live_mask, pre_act, hidden, partial_out)
    returned_out = lax.all_to_all(partial_out, "wide", split_axis=0, concat_axis=0, tiled=True)
    recv_cots = lax.all_to_all(
        pack_rows(out_cotangent), "wide", split_axis=0, concat_axis=0, tiled=True
    )
    grad_hidden = jnp.einsum(
        "rd,sd->rs", recv_cots, w_expert_out, preferred_element_type=jnp.float32
    )
    grad_pre = jnp.where(live_mask, grad_hidden * gelu_slope(pre_act), 0.0).astype(jnp.bfloat16)
    grad_second = jnp.einsum("rs,rd->sd", hidden, recv_cots, preferred_element_type=jnp.float32)
    grad_first = jnp.einsum("rd,rs->ds", recv_feats, grad_pre, preferred_element_type=jnp.float32)
    grad_bias = jnp.sum(grad_pre.astype(jnp.float32), axis=0)
    partial_back = jnp.einsum(
        "rs,ds->rd", grad_pre, w_expert_in, preferred_element_type=jnp.float32
    ).astype(jnp.bfloat16)
    grad_first, grad_second, grad_bias, partial_back = (
        grad_first,
        grad_second,
        grad_bias,
        partial_back,
    )
    returned_back = lax.all_to_all(partial_back, "wide", split_axis=0, concat_axis=0, tiled=True)
    pick_rows = (
        first_dest[:, None] + jnp.arange(owner_count, dtype=jnp.int32)[None, :]
    ) * slot_cap + block_rank[:, None]

    def unpack_rows(returned):
        rows = jnp.take(returned.reshape(slot_total, block_len * width), pick_rows, axis=0)
        return jnp.sum(rows.astype(jnp.float32), axis=1).reshape(points_local, width)

    layer_out = (point_feats.astype(jnp.float32) + attention + unpack_rows(returned_out)).astype(
        jnp.bfloat16
    )
    grad_feats = (
        out_cotangent.astype(jnp.float32) + attention_back + unpack_rows(returned_back)
    ).astype(jnp.bfloat16)
    share = DOMAIN_SPECIALS / total_points
    grad_first = grad_first * share
    grad_second = grad_second * share
    grad_bias = grad_bias * share
    sum_first, sum_second, sum_bias = (
        lax.psum(grad_first.astype(jnp.bfloat16), "narrow").astype(jnp.float32),
        lax.psum(grad_second.astype(jnp.bfloat16), "narrow").astype(jnp.float32),
        lax.psum(grad_bias.astype(jnp.bfloat16), "narrow").astype(jnp.float32),
    )
    narrow_index = lax.axis_index("narrow")
    feat_rows = width // narrow_count
    bias_rows = slab_cols // narrow_count
    grad_in = lax.dynamic_slice_in_dim(sum_first, narrow_index * feat_rows, feat_rows, 0)
    grad_out_w = lax.dynamic_slice_in_dim(sum_second, narrow_index * feat_rows, feat_rows, 1)
    grad_bias_out = lax.dynamic_slice_in_dim(sum_bias, narrow_index * bias_rows, bias_rows, 0)
    return (layer_out, grad_feats, grad_attention, grad_in, grad_out_w, grad_bias_out)


def solution(mesh):
    placed = (
        P(("wide", "narrow"), None),
        P(("wide", "narrow")),
        P(),
        P(),
        P(None, "wide"),
        P("wide"),
        P("wide", None),
        P(("wide", "narrow"), None),
    )
    return jax.shard_map(
        on_device,
        mesh=mesh,
        in_specs=placed,
        out_specs=(
            P(("wide", "narrow"), None),
            P(("wide", "narrow"), None),
            P(("wide", "narrow"), None),
            P("narrow", "wide"),
            P("wide", "narrow"),
            P(("wide", "narrow")),
        ),
        check_vma=False,
    )
```

profile of v0, /device:TPU:1, one launch (start us, length us, event | category | flops | bytes accessed | tf_op | source)
XLA Modules:
  0.0 706.8 jit_solution(7227469597073014413)
XLA Ops:
  11.8 16.3 %all-to-all-start = ((s32[128,2,1]{1,2,0:T(1,128)}), s32[128,2,1]{1,2,0:T(1,128)S(1)}, u32[]{:S(2)}, u32[]{:S(2)}) async-start(s32[128,2,1]{1,2,0:T(1,128)} %bitcast.7), calls=%async_computation | async-start | bytes 131072 | tf_op jit(solution)/shard_map/all_to_all | solution.py:137
  32.5 2.3 gather_fusion.3
  34.9 2.3 gather_fusion.1
  39.1 3.2 select_select_fusion
  42.5 2.5 all_to_all.36
  45.0 13.7 %all-to-all-start.1 = ((bf16[128,8,512]{2,1,0:T(8,128)(2,1)}), bf16[128,8,512]{2,1,0:T(8,128)(2,1)}, u32[]{:S(2)}, u32[]{:S(2)}) async-start(bf16[128,8,512]{2,1,0:T(8,128)(2,1)} %all_to_all.36), calls=%async_computation.1 | async-start | bytes 2097152 | tf_op jit(solution)/shard_map/all_to_all | solution.py:136
  62.0 2.5 all_to_all.41
  68.6 253.5 %all-reduce.9.cloned.1.call-done = (f32[8,64,64]{2,1,0:T(8,128)}, f32[8,64,64]{2,1,0:T(8,128)}) async-done(((f32[8,64,64]{2,1,0:T(8,128)}, f32[8,64,64]{2,1,0:T(8,128)}), (f32[8,64,64]{2,1,0:T(8,128)}, f32[8,64,64]{2,1,0:T(8,128)})) %all-reduce.9.cloned.1.call-update) | async-done | bytes 262160 | tf_op jit(solution)/shard_map/psum | solution.py:66
  326.2 12.4 %all-to-all-start.3 = ((bf16[128,8,512]{2,1,0:T(8,128)(2,1)}), bf16[128,8,512]{2,1,0:T(8,128)(2,1)}, u32[]{:S(2)}, u32[]{:S(2)}) async-start(bf16[128,8,512]{2,1,0:T(8,128)(2,1)} %all_to_all.41), calls=%async_computation.3 | async-start | bytes 2097152 | tf_op jit(solution)/shard_map/all_to_all | solution.py:148
  346.2 5.5 fusion
  355.3 10.7 %all-to-all-done.3 = bf16[128,8,512]{2,1,0:T(8,128)(2,1)} async-done(((bf16[128,8,512]{2,1,0:T(8,128)(2,1)}), bf16[128,8,512]{2,1,0:T(8,128)(2,1)}, u32[]{:S(2)}, u32[]{:S(2)}) %all-to-all-start.3) | async-done | bytes 1048608 | tf_op jit(solution)/shard_map/all_to_all | solution.py:148
  366.0 8.7 %all-to-all-start.2 = ((bf16[128,8,512]{2,1,0:T(8,128)(2,1)}), bf16[128,8,512]{2,1,0:T(8,128)(2,1)S(1)}, u32[]{:S(2)}, u32[]{:S(2)}) async-start(bf16[128,8,512]{2,1,0:T(8,128)(2,1)} %fusion.8), calls=%async_computation.2 | async-start | bytes 2097152 | tf_op jit(solution)/shard_map/all_to_all | solution.py:147
  377.2 2.5 maximum_multiply_fusion
  379.8 6.1 convert_reduce_fusion
  389.5 12.8 %all-to-all-done.2 = bf16[128,8,512]{2,1,0:T(8,128)(2,1)S(1)} async-done(((bf16[128,8,512]{2,1,0:T(8,128)(2,1)}), bf16[128,8,512]{2,1,0:T(8,128)(2,1)S(1)}, u32[]{:S(2)}, u32[]{:S(2)}) %all-to-all-start.2) | async-done | bytes 1048608 | tf_op jit(solution)/shard_map/all_to_all | solution.py:147
  402.3 9.2 %all-to-all-start.4 = ((bf16[128,8,512]{2,1,0:T(8,128)(2,1)}), bf16[128,8,512]{2,1,0:T(8,128)(2,1)}, u32[]{:S(2)}, u32[]{:S(2)}) async-start(bf16[128,8,512]{2,1,0:T(8,128)(2,1)} %fusion.9), calls=%async_computation.4 | async-start | bytes 2097152 | tf_op jit(solution)/shard_map/all_to_all | solution.py:167
  411.6 4.3 multiply_convert_fusion.1
  415.9 3.6 multiply_convert_fusion
  420.0 5.8 psum.39
  426.4 233.7 %all-reduce.7.cloned.1.call-done = f32[512,2048]{0,1:T(8,128)} async-done(((f32[512,2048]{0,1:T(8,128)}), f32[512,2048]{0,1:T(8,128)}) %all-reduce.7.cloned.1.call-update) | async-done | bytes 4194320
  669.8 2.3 reshape.275
  672.1 5.4 convert_reduce_fusion.1
  683.7 2.5 fusion.13
  686.1 10.0 %all-reduce.11.cloned.1.call-done = (bf16[512,1024]{1,0:T(8,128)(2,1)}, bf16[1024,512]{1,0:T(8,128)(2,1)}) async-done(((bf16[512,1024]{1,0:T(8,128)(2,1)}, bf16[1024,512]{1,0:T(8,128)(2,1)}), (bf16[512,1024]{1,0:T(8,128)(2,1)}, bf16[1024,512]{1,0:T(8,128)(2,1)})) %all-reduce.11.cloned.1.call-update) | async-done | bytes 2097168 | tf_op jit(solution)/shard_map/psum | solution.py:187
  (140 shorter events, 60.6 us)
Async XLA Ops:
  7.2 30.0 %copy-start = (bf16[512,1536]{1,0:T(8,128)(2,1)S(1)}, bf16[512,1536]{1,0:T(8,128)(2,1)}, u32[]{:S(2)}) copy-start(bf16[512,1536]{1,0:T(8,128)(2,1)} %param.14) | copy-start | bytes 4718596
  8.2 20.0 %copy-start.18 = (s32[64]{0:T(128)}, s32[64]{0:T(128)S(1)}, u32[]{:S(2)}) copy-start(s32[64]{0:T(128)S(1)} %convert_reduce_fusion.3) | copy-start | bytes 772
  8.8 19.3 %copy-start.20 = (s32[64]{0:T(128)}, s32[64]{0:T(128)S(1)}, u32[]{:S(2)}) copy-start(s32[64]{0:T(128)S(1)} %get-tuple-element.53) | copy-start | bytes 772
  11.8 33.2 %all-to-all-start = ((s32[128,2,1]{1,2,0:T(1,128)}), s32[128,2,1]{1,2,0:T(1,128)S(1)}, u32[]{:S(2)}, u32[]{:S(2)}) async-start(s32[128,2,1]{1,2,0:T(1,128)} %bitcast.7), calls=%async_computation | async-start | bytes 131072 | tf_op jit(solution)/shard_map/all_to_all | solution.py:137
  39.1 19.7 %copy-start.13 = (bf16[256,512]{1,0:T(8,128)(2,1)S(1)}, bf16[256,512]{1,0:T(8,128)(2,1)}, u32[]{:S(2)}) copy-start(bf16[256,512]{1,0:T(8,128)(2,1)} %convolution_convert_fusion.4) | copy-start | bytes 786436
  45.0 281.2 %all-to-all-start.1 = ((bf16[128,8,512]{2,1,0:T(8,128)(2,1)}), bf16[128,8,512]{2,1,0:T(8,128)(2,1)}, u32[]{:S(2)}, u32[]{:S(2)}) async-start(bf16[128,8,512]{2,1,0:T(8,128)(2,1)} %all_to_all.36), calls=%async_computation.1 | async-start | bytes 2097152 | tf_op jit(solution)/shard_map/all_to_all | solution.py:136
  58.7 263.4 %all-reduce.9.cloned.1.call-start = ((), (), s32[]{:S(2)}) async-start(), calls=%async_computation.6 | async-start | bytes 1048576 | tf_op jit(solution)/shard_map/psum | solution.py:66
  324.2 15.8 %copy-start.17 = (f32[256,8]{0,1:T(8,128)S(1)}, f32[256,8]{0,1:T(8,128)}, u32[]{:S(2)}) copy-start(f32[256,8]{0,1:T(8,128)} %copy-done.16) | copy-start | bytes 24580
  324.2 17.8 %copy-start.15 = (f32[256,8]{0,1:T(8,128)S(1)}, f32[256,8]{0,1:T(8,128)}, u32[]{:S(2)}) copy-start(f32[256,8]{0,1:T(8,128)} %copy-done.14) | copy-start | bytes 24580
  326.2 20.0 %copy-start.22 = (s32[1024]{0:T(1024)S(1)}, s32[1024]{0:T(1024)}, u32[]{:S(2)}) copy-start(s32[1024]{0:T(1024)} %eq.49) | copy-start | bytes 12292
  326.2 20.0 %copy-start.23 = (s32[1024]{0:T(1024)S(1)}, s32[1024]{0:T(1024)}, u32[]{:S(2)}) copy-start(s32[1024]{0:T(1024)} %add_select_fusion) | copy-start | bytes 12292
  326.2 20.0 %copy-start.27 = (f32[1024]{0:T(1024)S(1)}, f32[1024]{0:T(1024)}, u32[]{:S(2)}) copy-start(f32[1024]{0:T(1024)} %param.17) | copy-start | bytes 12292
  326.2 39.8 %all-to-all-start.3 = ((bf16[128,8,512]{2,1,0:T(8,128)(2,1)}), bf16[128,8,512]{2,1,0:T(8,128)(2,1)}, u32[]{:S(2)}, u32[]{:S(2)}) async-start(bf16[128,8,512]{2,1,0:T(8,128)(2,1)} %all_to_all.41), calls=%async_computation.3 | async-start | bytes 2097152 | tf_op jit(solution)/shard_map/all_to_all | solution.py:148
  353.0 21.7 %copy-start.11 = (f32[8,64,64]{2,1,0:T(8,128)S(1)}, f32[8,64,64]{2,1,0:T(8,128)}, u32[]{:S(2)}) copy-start(f32[8,64,64]{2,1,0:T(8,128)} %get-tuple-element.44) | copy-start | bytes 393220
  366.0 36.3 %all-to-all-start.2 = ((bf16[128,8,512]{2,1,0:T(8,128)(2,1)}), bf16[128,8,512]{2,1,0:T(8,128)(2,1)S(1)}, u32[]{:S(2)}, u32[]{:S(2)}) async-start(bf16[128,8,512]{2,1,0:T(8,128)(2,1)} %fusion.8), calls=%async_computation.2 | async-start | bytes 2097152 | tf_op jit(solution)/shard_map/all_to_all | solution.py:147
  374.7 285.4 %all-reduce.7.cloned.1.call-start = ((), (), s32[]{:S(2)}) async-start(), calls=%async_computation.5 | async-start | bytes 8388608
  402.3 17.2 %copy-start.2 = (bf16[128,8,512]{2,1,0:T(8,128)(2,1)}, bf16[128,8,512]{2,1,0:T(8,128)(2,1)S(1)}, u32[]{:S(2)}) copy-start(bf16[128,8,512]{2,1,0:T(8,128)(2,1)S(1)} %all-to-all-done.2) | copy-start | bytes 3145732
  402.3 264.1 %all-to-all-start.4 = ((bf16[128,8,512]{2,1,0:T(8,128)(2,1)}), bf16[128,8,512]{2,1,0:T(8,128)(2,1)}, u32[]{:S(2)}, u32[]{:S(2)}) async-start(bf16[128,8,512]{2,1,0:T(8,128)(2,1)} %fusion.9), calls=%async_computation.4 | async-start | bytes 2097152 | tf_op jit(solution)/shard_map/all_to_all | solution.py:167
  411.5 284.6 %all-reduce.11.cloned.1.call-start = ((), (), s32[]{:S(2)}) async-start(), calls=%async_computation.7 | async-start | bytes 4194304 | tf_op jit(solution)/shard_map/psum | solution.py:187
  668.1 13.5 %copy-start.5 = (bf16[8,64,256]{2,1,0:T(8,128)(2,1)S(1)}, bf16[8,64,256]{2,1,0:T(8,128)(2,1)}, u32[]{:S(2)}) copy-start(bf16[8,64,256]{2,1,0:T(8,128)(2,1)} %copy-done.4) | copy-start | bytes 786436
  669.8 11.7 %copy-start.7 = (bf16[512,512]{1,0:T(8,128)(2,1)S(1)}, bf16[512,512]{1,0:T(8,128)(2,1)}, u32[]{:S(2)}) copy-start(bf16[512,512]{1,0:T(8,128)(2,1)} %param.15) | copy-start | bytes 1572868
  669.8 13.8 %copy-start.6 = (bf16[256,512]{1,0:T(8,128)(2,1)S(1)}, bf16[256,512]{1,0:T(8,128)(2,1)}, u32[]{:S(2)}) copy-start(bf16[256,512]{1,0:T(8,128)(2,1)} %param.19) | copy-start | bytes 786436
  669.8 13.8 %copy-start.10 = (bf16[8,64,256]{2,1,0:T(8,128)(2,1)S(1)}, bf16[8,64,256]{2,1,0:T(8,128)(2,1)}, u32[]{:S(2)}) copy-start(bf16[8,64,256]{2,1,0:T(8,128)(2,1)} %copy-done.9) | copy-start | bytes 786436
  669.8 13.8 %copy-start.12 = (bf16[256,8,64]{0,2,1:T(8,128)(2,1)S(1)}, bf16[256,8,64]{0,2,1:T(8,128)(2,1)}, u32[]{:S(2)}) copy-start(bf16[256,8,64]{0,2,1:T(8,128)(2,1)} %divide_convert_fusion) | copy-start | bytes 786436
  (14 other events, 55.6 us)
Sparse Core Ops, SparseCore 0:
  65.7 256.3 all-reduce.8
  381.0 279.0 all-reduce.6
  662.7 33.3 all-reduce.10
where the time goes:
time: 708 us; the launch traced here: 707 us
  waiting for transfers between devices  521 us (74%)
  starting transfers between devices  60.5 us (9%)
  matrix products  42.6 us (6%)
  local copies, waits for them, and re-layouts  39.3 us (6%)
  other arithmetic  23.6 us (3%)
  between operations  14.3 us (2%)
    psum x1, waiting for transfers between devices, on_device(): lax.psum((local_summary, local_grad), ('wide', 'narrow'))  254 us
    unnamed x4, waiting for transfers between devices  234 us
    all_to_all x1, starting transfers between devices, on_device(): lax.all_to_all(send_labels, 'wide', split_axis=0, concat_axis=0, tiled=True)  16.3 us
  transfers between devices with their start and end apart: 8, of which 5 were waited for; matrix products, arithmetic and copies ran while one was open for 12% of the time, Pallas kernels for 0%

commit v1 on v0

v1 whole, which is shorter than its diff:
```python
import jax
import jax.numpy as jnp
from jax import lax
from jax.experimental import pallas as pl
from jax.experimental.pallas import tpu as pltpu
from jax.sharding import PartitionSpec as P

F32 = jnp.float32
BF = jnp.bfloat16
EPS = 1e-05
GS = 0.7978845608
GC = 0.044715
W = 512
PTS = 256
NB = 64
CHIPS = 128
TOTAL = 65536.0
SHARE = 64.0 / 65536.0
HALF = 1024
VM = pl.BlockSpec(memory_space=pltpu.VMEM)
SM = pl.BlockSpec(memory_space=pltpu.SMEM)


def mm(a, b):
    return jnp.dot(a, b, preferred_element_type=F32)


def mm_t(a, b):
    return lax.dot_general(a, b, (((1,), (1,)), ((), ())), preferred_element_type=F32)


def t_mm(a, b):
    return lax.dot_general(a, b, (((0,), (0,)), ((), ())), preferred_element_type=F32)


def head_ones():
    r = lax.broadcasted_iota(jnp.int32, (W, W), 0) // 64
    c = lax.broadcasted_iota(jnp.int32, (W, W), 1) // 64
    return jnp.where(r == c, 1.0 / 64.0, 0.0).astype(BF)


def head_mean(v, ones):
    hi = v.astype(BF)
    lo = (v - hi.astype(F32)).astype(BF)
    return mm(hi, ones) + mm(lo, ones)


def normalize(raw, ones):
    cen = raw.astype(F32) - mm(raw, ones)
    scale = jnp.sqrt(head_mean(cen * cen, ones) + EPS)
    return cen / scale, scale


def low_rows(shape):
    return lax.broadcasted_iota(jnp.int32, shape, 0) < 4


def call(body, outs, scratch=(), smem_in=(), n_in=0, smem_out=(), cost=None, name=None):
    return pl.pallas_call(
        body,
        out_shape=outs,
        in_specs=[SM if i in smem_in else VM for i in range(n_in)],
        out_specs=[SM if i in smem_out else VM for i in range(len(outs))],
        scratch_shapes=list(scratch),
        cost_estimate=cost,
        name=name,
        compiler_params=pltpu.CompilerParams(vmem_limit_bytes=56 * 1024 * 1024),
    )


def cost(us):
    return pl.CostEstimate(flops=int(us * 1e9), bytes_accessed=int(us * 1e6), transcendentals=0)


def sds(shape, dtype):
    return jax.ShapeDtypeStruct(shape, dtype)


def front_kernel(ids, x_ref, c_ref, wq_ref, wo_ref, send, slots, qkv_ref, g_ref, cnt, ss):
    @pl.loop(0, NB)
    def _(i):
        cnt[i] = 0

    @pl.loop(0, NB)
    def _(b):
        r = ids[b]
        k = cnt[r]
        cnt[r] = k + 1
        slots[b] = 2 * r + k

    send[:, :, 0:W] = jnp.zeros((CHIPS, 8, W), BF)
    low = low_rows((8, W))

    @pl.loop(0, 16)
    def _(i):
        x = x_ref[pl.ds(pl.multiple_of(i * 16, 16), 16), :].astype(F32)
        c = c_ref[pl.ds(pl.multiple_of(i * 16, 16), 16), :].astype(F32)
        for h in range(2):
            xa, ca = x[8 * h : 8 * h + 8], c[8 * h : 8 * h + 8]
            xr, cr = pltpu.roll(xa, 4, 0), pltpu.roll(ca, 4, 0)
            send[slots[4 * i + 2 * h], :, 0:W] = jnp.where(low, xa, cr).astype(BF)
            send[slots[4 * i + 2 * h + 1], :, 0:W] = jnp.where(low, xr, ca).astype(BF)

    ones = head_ones()
    qkv = mm(x_ref[...], wq_ref[...]).astype(BF)
    qkv_ref[...] = qkv
    g = mm_t(c_ref[...], wo_ref[...]).astype(BF)
    g_ref[...] = g
    kn = normalize(qkv[:, W : 2 * W], ones)[0].astype(BF)
    vn = normalize(qkv[:, 2 * W :], ones)[0].astype(BF)
    left = lax.broadcasted_iota(jnp.int32, (64, 128), 1) < 64
    for j in range(4):
        s = slice(128 * j, 128 * j + 128)
        a = t_mm(kn[:, s], vn[:, s])
        ss[64 * j : 64 * j + 64, :] = jnp.where(left, a[:64], a[64:])
        a = t_mm(qkv[:, s], g[:, s])
        ss[256 + 64 * j : 320 + 64 * j, :] = jnp.where(left, a[:64], a[64:])
    low2 = low_rows((8, 128))

    @pl.loop(0, 64)
    def _(i):
        v = ss[pl.ds(pl.multiple_of(i * 8, 8), 8), :]
        hi = v.astype(BF).astype(F32)
        lo = v - hi
        send[2 * i, :, W:] = jnp.where(low2, hi, pltpu.roll(lo, 4, 0)).astype(BF)
        send[2 * i + 1, :, W:] = jnp.where(low2, pltpu.roll(hi, 4, 0), lo).astype(BF)


def chunk_kernel(recv, out):
    v = jnp.sum(recv[:, :, W:].astype(F32), axis=0)
    out[...] = v + pltpu.roll(v, 4, 0)


def spread_kernel(a_ref, b_ref, out):
    v = ((a_ref[...] + b_ref[...]) * (1.0 / TOTAL)).astype(BF)
    out[...] = jnp.broadcast_to(v[None], (CHIPS, 8, 128))


def expert_kernel(
    n_ref, recv, wi, wiy, win, wo, woy, won, b_ref, bp_ref, send, x_s, c_s, hid, gpre, o_s, k_s
):
    n = n_ref[0]
    mine = pl.ds(pl.multiple_of(n * 256, 256), 256)
    other = pl.ds(pl.multiple_of(256 - n * 256, 256), 256)
    low = low_rows((8, W))

    @pl.loop(0, 32)
    def _(i):
        xs, cs = [], []
        for h in range(2):
            a = recv[4 * i + 2 * h, :, 0:W].astype(F32)
            b = recv[4 * i + 2 * h + 1, :, 0:W].astype(F32)
            xs.append(jnp.where(low, a, pltpu.roll(b, 4, 0)))
            cs.append(jnp.where(low, pltpu.roll(a, 4, 0), b))
        rows = pl.ds(pl.multiple_of(i * 16, 16), 16)
        x_s[rows, :] = jnp.concatenate(xs, axis=0).astype(BF)
        c_s[rows, :] = jnp.concatenate(cs, axis=0).astype(BF)

    def act(pre, gh, cols):
        sq = pre * pre
        t = jnp.tanh(GS * (pre + GC * pre * sq))
        up = 0.5 * (1.0 + t)
        hid[:, cols] = (pre * up).astype(BF)
        slope = up + 0.5 * pre * (1.0 - t * t) * GS * (1.0 + 3.0 * GC * sq)
        gpre[:, cols] = (gh * slope).astype(BF)

    @pl.loop(0, 4)
    def _(i):
        cols = pl.ds(pl.multiple_of(i * 256, 256), 256)
        pre = mm(x_s[...], wi[:, cols]) + b_ref[:, cols]
        gh = mm_t(c_s[...], wo[cols, :])
        act(pre, gh, cols)

    @pl.loop(0, 4)
    def _(i):
        cols = pl.ds(pl.multiple_of(i * 256, 256), 256)
        pre = mm(x_s[:, mine], wiy[:, cols]) + mm(x_s[:, other], win[:, cols]) + bp_ref[:, cols]
        gh = mm_t(c_s[:, mine], woy[cols, :]) + mm_t(c_s[:, other], won[cols, :])
        act(pre, gh, pl.ds(pl.multiple_of(HALF + i * 256, 256), 256))

    for yr, kr, part in ((woy, wiy, mine), (won, win, other)):
        o_s[:, part] = mm(hid[:, :HALF], wo[:, part]) + mm(hid[:, HALF:], yr[...])
        k_s[:, part] = mm_t(gpre[:, :HALF], wi[part, :]) + mm_t(gpre[:, HALF:], kr[...])

    @pl.loop(0, 64)
    def _(i):
        rows = pl.ds(pl.multiple_of(i * 8, 8), 8)
        o, k = o_s[rows, :], k_s[rows, :]
        send[2 * i, :, :] = jnp.where(low, o, pltpu.roll(k, 4, 0)).astype(BF)
        send[2 * i + 1, :, :] = jnp.where(low, pltpu.roll(o, 4, 0), k).astype(BF)


def weight_kernel(n_ref, x_s, c_s, hid, gpre, keep_i, send_i, keep_o, send_o):
    n = n_ref[0]
    mine = pl.ds(pl.multiple_of(n * 256, 256), 256)
    other = pl.ds(pl.multiple_of(256 - n * 256, 256), 256)

    @pl.loop(0, 4)
    def _(i):
        cols = pl.ds(pl.multiple_of(i * 512, 512), 512)
        g = gpre[:, cols]
        keep_i[0:256, cols] = t_mm(x_s[:, mine], g) * SHARE
        send_i[0:256, cols] = (t_mm(x_s[:, other], g) * SHARE).astype(BF)
        bias = jnp.sum(g.astype(F32), axis=0, keepdims=True) * SHARE
        keep_i[256:272, cols] = jnp.broadcast_to(bias, (16, 512))
        send_i[256:272, cols] = jnp.broadcast_to(bias, (16, 512)).astype(BF)
        h = hid[:, cols]
        keep_o[cols, :] = t_mm(h, c_s[:, mine]) * SHARE
        send_o[cols, :] = (t_mm(h, c_s[:, other]) * SHARE).astype(BF)


def attn_kernel(
    n_ref, rs, qkv_ref, g_ref, x_ref, c_ref, wq_ref, wo_ref, base_o, base_k, keep, send, ss, gq
):
    n = n_ref[0]
    low = low_rows((8, 128))

    @pl.loop(0, 32)
    def _(i):
        t = [
            jnp.where(low, rs[4 * i + 2 * h].astype(F32), rs[4 * i + 2 * h + 1].astype(F32))
            for h in range(2)
        ]
        ss[pl.ds(pl.multiple_of(i * 16, 16), 16), :] = jnp.concatenate(t, axis=0).astype(BF)

    ones = head_ones()
    qkv, g = qkv_ref[...], g_ref[...]
    ku, ks = normalize(qkv[:, W : 2 * W], ones)
    vu, vs = normalize(qkv[:, 2 * W :], ones)
    kn, vn = ku.astype(BF), vu.astype(BF)
    left = lax.broadcasted_iota(jnp.int32, (64, 128), 1) < 64

    def diag(p):
        z = jnp.zeros_like(p)
        return jnp.concatenate([jnp.where(left, p, z), jnp.where(left, z, p)], axis=0)

    mixed, gk, gv = [], [], []
    for j in range(4):
        s = slice(128 * j, 128 * j + 128)
        sm = diag(ss[64 * j : 64 * j + 64, :].astype(F32)).astype(BF)
        gs = diag(ss[256 + 64 * j : 320 + 64 * j, :].astype(F32)).astype(BF)
        mixed.append(mm(qkv[:, s], sm).astype(BF))
        gq[:, s] = mm_t(g[:, s], sm).astype(BF)
        gk.append(mm_t(vn[:, s], gs))
        gv.append(mm(kn[:, s], gs))
    mixed = jnp.concatenate(mixed, axis=1)

    def back(gr, u, sc):
        return ((gr - head_mean(gr, ones) - u * head_mean(gr * u, ones)) / sc).astype(BF)

    gq[:, W : 2 * W] = back(jnp.concatenate(gk, axis=1), ku, ks)
    gq[:, 2 * W :] = back(jnp.concatenate(gv, axis=1), vu, vs)
    x, c = x_ref[...], c_ref[...]
    base_o[...] = x.astype(F32) + mm(mixed, wo_ref[...])
    base_k[...] = c.astype(F32) + mm_t(gq[...], wq_ref[...])

    def pick(core):
        r = lax.broadcasted_iota(jnp.int32, (W, PTS), 0)
        k = lax.broadcasted_iota(jnp.int32, (W, PTS), 1)
        return jnp.where(r == 4 * (k // 2) + 2 * core + k % 2, 1.0, 0.0).astype(BF)

    for core, dst in ((n, keep), (1 - n, send)):
        sel = pick(core)
        xk, mk = mm(x, sel).astype(BF), mm(mixed, sel).astype(BF)
        for q in range(3):
            cols = slice(W * q, W * q + W)
            dst[:, cols] = (t_mm(xk, gq[:, cols]) * (1.0 / TOTAL)).astype(dst.dtype)
        dst[:, 3 * W :] = (t_mm(mk, c) * (1.0 / TOTAL)).astype(dst.dtype)


def deal_kernel(keep, recv, out):
    r = lax.broadcasted_iota(jnp.int32, (2 * W, PTS), 0)
    k = lax.broadcasted_iota(jnp.int32, (2 * W, PTS), 1)
    acc = None
    for q in range(4):
        cols = slice(W * q, W * q + W)
        v = (keep[:, cols] + recv[:, cols].astype(F32)).astype(BF)
        part = mm(jnp.where(r == 4 * k + q, 1.0, 0.0).astype(BF), v)
        acc = part if acc is None else acc + part
    out[...] = acc.astype(BF)


def total_kernel(recv, out):
    out[...] = jnp.sum(recv[...].astype(F32), axis=0)


def final_kernel(slots, ret, base_o, base_k, lo, gf):
    low = low_rows((8, W))

    @pl.loop(0, 16)
    def _(i):
        os, ks = [], []
        for h in range(2):
            a = ret[slots[4 * i + 2 * h]].astype(F32)
            b = ret[slots[4 * i + 2 * h + 1]].astype(F32)
            os.append(jnp.where(low, a, pltpu.roll(b, 4, 0)))
            ks.append(jnp.where(low, pltpu.roll(a, 4, 0), b))
        rows = pl.ds(pl.multiple_of(i * 16, 16), 16)
        lo[rows, :] = (base_o[rows, :] + jnp.concatenate(os, axis=0)).astype(BF)
        gf[rows, :] = (base_k[rows, :] + jnp.concatenate(ks, axis=0)).astype(BF)


def on_device(x, ids, wq, wo_att, wi, bi, wo, c):
    n = lax.axis_index("narrow")
    nv = n.reshape(1).astype(jnp.int32)
    pair = [(i, i ^ 1) for i in range(CHIPS)]
    swap = [(0, 1), (1, 0)]

    def across(v):
        return lax.ppermute(v, "wide", pair)

    def beside(v):
        return lax.ppermute(v, "narrow", swap)

    def deal(v):
        return lax.all_to_all(v, "wide", split_axis=0, concat_axis=0, tiled=True)

    wiy = across(lax.dynamic_slice_in_dim(wi, n * 256, 256, 0))
    woy = across(lax.dynamic_slice_in_dim(wo, n * 256, 256, 1))
    bp = across(bi)
    win, won = beside(wiy), beside(woy)

    send, slots, qkv, g = call(
        front_kernel,
        [sds((CHIPS, 8, 640), BF), sds((NB,), jnp.int32), sds((PTS, 3 * W), BF), sds((PTS, W), BF)],
        [pltpu.SMEM((NB,), jnp.int32), pltpu.VMEM((W, 128), F32)],
        smem_in=(0,), n_in=5, smem_out=(1,), cost=cost(5), name="front",
    )(ids, x, c, wq, wo_att)
    recv = deal(send)
    (chunk,) = call(chunk_kernel, [sds((8, 128), F32)], n_in=1, cost=cost(1), name="chunk")(recv)
    (spread,) = call(spread_kernel, [sds((CHIPS, 8, 128), BF)], n_in=2, cost=cost(1), name="spread")(
        chunk, beside(chunk)
    )
    rs = deal(spread)
    ret, x_s, c_s, hid, gpre = call(
        expert_kernel,
        [sds((CHIPS, 8, W), BF), sds((W, W), BF), sds((W, W), BF), sds((W, 2 * HALF), BF), sds((W, 2 * HALF), BF)],
        [pltpu.VMEM((W, W), F32), pltpu.VMEM((W, W), F32)],
        smem_in=(0,), n_in=10, cost=cost(12), name="expert",
    )(nv, recv, wi, wiy, win, wo, woy, won, bi.reshape(1, HALF), bp.reshape(1, HALF))
    back = deal(ret)
    base_o, base_k, keep, away = call(
        attn_kernel,
        [sds((PTS, W), F32), sds((PTS, W), F32), sds((PTS, 4 * W), F32), sds((PTS, 4 * W), BF)],
        [pltpu.VMEM((W, 128), BF), pltpu.VMEM((PTS, 3 * W), BF)],
        smem_in=(0,), n_in=8, cost=cost(7), name="attn",
    )(nv, rs, qkv, g, x, c, wq, wo_att)
    (att_send,) = call(deal_kernel, [sds((2 * W, W), BF)], n_in=2, cost=cost(2), name="deal")(
        keep, beside(away)
    )
    att_recv = deal(att_send.reshape(CHIPS, 8, W))
    keep_i, send_i, keep_o, send_o = call(
        weight_kernel,
        [sds((272, 2 * HALF), F32), sds((272, 2 * HALF), BF), sds((2 * HALF, 256), F32), sds((2 * HALF, 256), BF)],
        smem_in=(0,), n_in=5, cost=cost(7), name="weight",
    )(nv, x_s, c_s, hid, gpre)
    sum_i = keep_i + beside(send_i).astype(F32)
    sum_o = keep_o + beside(send_o).astype(F32)
    tot_i = sum_i[:, :HALF] + across(sum_i[:, HALF:].astype(BF)).astype(F32)
    tot_o = sum_o[:HALF] + across(sum_o[HALF:].astype(BF)).astype(F32)
    grad_in = tot_i[:256]
    grad_b = lax.dynamic_slice_in_dim(tot_i[256], n * 512, 512, 0)
    layer_out, grad_feats = call(
        final_kernel, [sds((PTS, W), BF), sds((PTS, W), BF)], smem_in=(0,), n_in=4, cost=cost(2), name="final"
    )(slots, back, base_o, base_k)
    (att,) = call(total_kernel, [sds((8, W), F32)], n_in=1, cost=cost(1), name="total")(att_recv)
    return (layer_out, grad_feats, att.reshape(2, 4 * W), grad_in, tot_o, grad_b)


def solution(mesh):
    placed = (
        P(("wide", "narrow"), None),
        P(("wide", "narrow")),
        P(),
        P(),
        P(None, "wide"),
        P("wide"),
        P("wide", None),
        P(("wide", "narrow"), None),
    )
    return jax.shard_map(
        on_device,
        mesh=mesh,
        in_specs=placed,
        out_specs=(
            P(("wide", "narrow"), None),
            P(("wide", "narrow"), None),
            P(("wide", "narrow"), None),
            P("narrow", "wide"),
            P("wide", "narrow"),
            P(("wide", "narrow")),
        ),
        check_vma=False,
    )
```

time: 708 us -> 193 us (0.27)
  waiting for transfers between devices: 521 us -> 70.6 us
  Pallas kernels: 0 us -> 49.4 us
  matrix products: 42.6 us -> 0 us
  local copies, waits for them, and re-layouts: 39.3 us -> 7.71 us
  other arithmetic: 23.6 us -> 4.51 us
  between operations: 14.3 us -> 0.88 us
    psum x2 -> x0, waiting for transfers between devices: 264 us -> none  [the longest x1 254 us: on_device(): lax.psum((local_summary, local_grad), ('wide', 'narrow'))]
    unnamed x4 -> x0, waiting for transfers between devices: 234 us -> none
    ppermute x0 -> x11, waiting for transfers between devices: none -> 64.8 us  [the longest x5 64 us: across(): return lax.ppermute(v, 'wide', pair)]
    pallas_call x0 -> x9, Pallas kernels: none -> 49.4 us  [the longest x1 13.9 us: on_device(): call(expert_kernel, [sds((CHIPS, 8, W), BF), sds((W, W), BF), sds((W, W),...]
    dot_general x18 -> x0, matrix products: 42.6 us -> none  [the longest x1 6.11 us: on_device(): jnp.einsum('rd,sd->rs', recv_cots, w_expert_out, preferred_element_type=j...]
    all_to_all x5 -> x4, waiting for transfers between devices: 23.6 us -> 5.73 us  [deal(): return lax.all_to_all(v, 'wide', split_axis=0, concat_axis=0, tiled=True)]
    gather x7 -> x0, local copies, waits for them, and re-layouts: 12.6 us -> none  [the longest x4 6.09 us: unpack_rows(): jnp.take(returned.reshape(slot_total, block_len * width), pick_rows, axis=0)]
    all_to_all x5 -> x4, starting transfers between devices: 60.3 us -> 51 us  [deal(): return lax.all_to_all(v, 'wide', split_axis=0, concat_axis=0, tiled=True)]
  transfers between devices with their start and end apart: 8 -> 15, of which waited for: 5 -> 6; matrix products, arithmetic and copies ran while one was open for 12% -> 4% of each run, Pallas kernels for 0% -> 21%
where the time goes in v1:
time: 193 us
  waiting for transfers between devices  70.6 us (37%)
  starting transfers between devices  59.7 us (31%)
  Pallas kernels  49.4 us (26%)
  local copies, waits for them, and re-layouts  7.71 us (4%)
  other arithmetic  4.51 us (2%)
    ppermute x5, waiting for transfers between devices, across(): return lax.ppermute(v, 'wide', pair)  64 us
    all_to_all x4, starting transfers between devices, deal(): return lax.all_to_all(v, 'wide', split_axis=0, concat_axis=0, tiled=True)  51 us
    pallas_call x1, Pallas kernels, on_device(): call(expert_kernel, [sds((CHIPS, 8, W), BF), sds((W, W), BF), sds((W, W),...  13.9 us
    pallas_call x1, Pallas kernels, on_device(): call(attn_kernel, [sds((PTS, W), F32), sds((PTS, W), F32), sds((PTS, 4 *...  8.03 us
    pallas_call x1, Pallas kernels, on_device(): call(weight_kernel, [sds((272, 2 * HALF), F32), sds((272, 2 * HALF), BF),...  7.92 us
    pallas_call x1, Pallas kernels, on_device(): call(front_kernel, [sds((CHIPS, 8, 640), BF), sds((NB,), jnp.int32), sds(...  7.28 us
    all_to_all x4, waiting for transfers between devices, deal(): return lax.all_to_all(v, 'wide', split_axis=0, concat_axis=0, tiled=True)  5.73 us
    ppermute x6, starting transfers between devices, beside(): return lax.ppermute(v, 'narrow', swap)  5.03 us
  transfers between devices with their start and end apart: 15, of which 6 were waited for; matrix products, arithmetic and copies ran while one was open for 4% of the time, Pallas kernels for 21%

profile of v1, /device:TPU:1, one launch (start us, length us, event | category | flops | bytes accessed | tf_op | source)
XLA Modules:
  0.0 192.7 jit_solution(10453593840273842590)
XLA Ops:
  0.6 7.3 %front.1 = (bf16[128,8,640]{2,1,0:T(8,128)(2,1)}, s32[64]{0:T(128)}, bf16[256,1536]{1,0:T(8,128)(2,1)}, bf16[256,512]{1,0:T(8,128)(2,1)}) custom-call(s32[64]{0:T(128)} %ids.1, bf16[256,512]{1,0:T(8,128)(2,1)} %x_ref.3, bf16[256,512]{1,0:T(8,128)(2,1)} %c_ref.3, bf16[512,1536]{1,0:T(8,128)(2,1)} %wq_ref.3, bf16[512,512]{1,0:T(8,128)(2,1)} %wo_ref.3), custom_call_target="tpu_custom_call" | custom-call | flops 5000000000 | bytes 5000000 | tf_op jit(solution)/shard_map/front/pallas_call | solution.py:323
  7.9 16.5 %all-to-all-start = ((bf16[128,8,640]{2,1,0:T(8,128)(2,1)}), bf16[128,8,640]{2,1,0:T(8,128)(2,1)S(1)}, u32[]{:S(2)}, u32[]{:S(2)}) async-start(bf16[128,8,640]{2,1,0:T(8,128)(2,1)} %get-tuple-element.26), calls=%async_computation | async-start | bytes 2621440 | tf_op jit(solution)/shard_map/all_to_all | solution.py:316
  26.2 21.5 %collective-permute-done.wiy = bf16[256,1024]{1,0:T(8,128)(2,1)S(1)} collective-permute-done((bf16[256,1024]{1,0:T(8,128)(2,1)S(1)}, bf16[256,1024]{1,0:T(8,128)(2,1)S(1)}, u32[]{:S(2)}, u32[]{:S(2)}) %collective-permute-start) | collective-permute-done | bytes 524320 | tf_op jit(solution)/shard_map/ppermute | solution.py:310
  47.7 2.6 %collective-permute-start.1 = (bf16[256,1024]{1,0:T(8,128)(2,1)S(1)}, bf16[256,1024]{1,0:T(8,128)(2,1)S(1)}, u32[]{:S(2)}, u32[]{:S(2)}) collective-permute-start(bf16[256,1024]{1,0:T(8,128)(2,1)S(1)} %collective-permute-done.wiy), channel_id=1, source_target_pairs={{0,1},{1,0},{2,3},{3,2},{4,5},{5,4},{6,7},{7,6},{8,9},{9,8},{10,11... | collective-permute-start | bytes 1572872 | tf_op jit(solution)/shard_map/ppermute | solution.py:313
  50.3 12.7 %collective-permute-done.2.woy = bf16[1024,256]{1,0:T(8,128)(2,1)S(1)} collective-permute-done((bf16[1024,256]{1,0:T(8,128)(2,1)S(1)}, bf16[1024,256]{1,0:T(8,128)(2,1)S(1)}, u32[]{:S(2)}, u32[]{:S(2)}) %collective-permute-start.2) | collective-permute-done | bytes 524320 | tf_op jit(solution)/shard_map/ppermute | solution.py:310
  63.9 1.1 copy-done.3
  64.9 2.0 %chunk.1.a_ref = f32[8,128]{1,0:T(8,128)} custom-call(bf16[128,8,640]{2,1,0:T(8,128)(2,1)} %copy-done.3), custom_call_target="tpu_custom_call" | custom-call | flops 1000000000 | bytes 1000000 | tf_op jit(solution)/shard_map/chunk/pallas_call | solution.py:330
  69.0 1.4 spread.1
  70.4 12.5 %all-to-all-start.2 = ((bf16[128,8,128]{2,1,0:T(8,128)(2,1)}), bf16[128,8,128]{2,1,0:T(8,128)(2,1)S(1)}, u32[]{:S(2)}, u32[]{:S(2)}) async-start(bf16[128,8,128]{2,1,0:T(8,128)(2,1)} %spread.1), calls=%async_computation.2 | async-start | bytes 524288 | tf_op jit(solution)/shard_map/all_to_all | solution.py:316
  83.9 13.9 %expert.1 = (bf16[128,8,512]{2,1,0:T(8,128)(2,1)}, bf16[512,512]{1,0:T(8,128)(2,1)}, bf16[512,512]{1,0:T(8,128)(2,1)}, bf16[512,2048]{1,0:T(8,128)(2,1)}, bf16[512,2048]{1,0:T(8,128)(2,1)}) custom-call(s32[1]{0:T(128)} %bitcast.n_ref, bf16[128,8,640]{2,1,0:T(8,128)(2,1)} %copy-done.3, bf16[512,1024]{1,0:T(8,128)(2,1)} %wi.1, bf16[256,1024]{1,0:T(8,128)(2,1)} %copy-done.8, ...), custom_call_target="tpu_custom_call" | custom-call | flops 12000000000 | bytes 12000000 | tf_op jit(solution)/shard_map/expert/pallas_call | solution.py:335
  97.8 13.6 %all-to-all-start.1 = ((bf16[128,8,512]{2,1,0:T(8,128)(2,1)}), bf16[128,8,512]{2,1,0:T(8,128)(2,1)}, u32[]{:S(2)}, u32[]{:S(2)}) async-start(bf16[128,8,512]{2,1,0:T(8,128)(2,1)} %get-tuple-element.27), calls=%async_computation.1 | async-start | bytes 2097152 | tf_op jit(solution)/shard_map/all_to_all | solution.py:316
  111.4 8.0 %attn.1 = (f32[256,512]{1,0:T(8,128)}, f32[256,512]{1,0:T(8,128)}, f32[256,2048]{1,0:T(8,128)}, bf16[256,2048]{1,0:T(8,128)(2,1)}) custom-call(s32[1]{0:T(128)} %bitcast.n_ref, bf16[128,8,128]{2,1,0:T(8,128)(2,1)} %copy-done.4, bf16[256,1536]{1,0:T(8,128)(2,1)} %get-tuple-element.28.qkv_ref, bf16[256,512]{1,0:T(8,128)(2,1)} %get-tuple-element.29.g_ref, ...), custom_call_target="tpu_custom_call" | custom-call | flops 7000000000 | bytes 7000000 | tf_op jit(solution)/shard_map/attn/pallas_call | solution.py:342
  120.5 7.9 %weight.1 = (f32[272,2048]{1,0:T(8,128)}, bf16[272,2048]{1,0:T(8,128)(2,1)}, f32[2048,256]{1,0:T(8,128)}, bf16[2048,256]{1,0:T(8,128)(2,1)}) custom-call(s32[1]{0:T(128)} %bitcast.n_ref, bf16[512,512]{1,0:T(8,128)(2,1)} %get-tuple-element.36.x_s, bf16[512,512]{1,0:T(8,128)(2,1)} %get-tuple-element.37.c_s, bf16[512,2048]{1,0:T(8,128)(2,1)} %get-tuple-element.38.hid, ...), custom_call_target="tpu_custom_call" | custom-call | flops 7000000000 | bytes 7000000 | tf_op jit(solution)/shard_map/weight/pallas_call | solution.py:352
  129.9 4.1 %deal.1 = bf16[1024,512]{1,0:T(8,128)(2,1)} custom-call(f32[256,2048]{1,0:T(8,128)} %get-tuple-element.34.keep, bf16[256,2048]{1,0:T(8,128)(2,1)} %copy-done.7), custom_call_target="tpu_custom_call" | custom-call | flops 2000000000 | bytes 2000000 | tf_op jit(solution)/shard_map/deal/pallas_call | solution.py:348
  134.0 5.7 %all-to-all-done.1.ret = bf16[128,8,512]{2,1,0:T(8,128)(2,1)} async-done(((bf16[128,8,512]{2,1,0:T(8,128)(2,1)}), bf16[128,8,512]{2,1,0:T(8,128)(2,1)}, u32[]{:S(2)}, u32[]{:S(2)}) %all-to-all-start.1) | async-done | bytes 1048608 | tf_op jit(solution)/shard_map/all_to_all | solution.py:316
  139.7 8.5 %all-to-all-start.3 = ((bf16[128,8,512]{2,1,0:T(8,128)(2,1)}), bf16[128,8,512]{2,1,0:T(8,128)(2,1)}, u32[]{:S(2)}, u32[]{:S(2)}) async-start(bf16[128,8,512]{2,1,0:T(8,128)(2,1)} %bitcast.5), calls=%async_computation.3 | async-start | bytes 2097152 | tf_op jit(solution)/shard_map/all_to_all | solution.py:316
  148.3 1.6 convert_add_fusion.1
  152.8 18.9 %collective-permute-done.10 = bf16[1024,256]{1,0:T(8,128)(2,1)} collective-permute-done((bf16[1024,256]{1,0:T(8,128)(2,1)}, bf16[1024,256]{1,0:T(8,128)(2,1)}, u32[]{:S(2)}, u32[]{:S(2)}) %collective-permute-start.10) | collective-permute-done | bytes 524320 | tf_op jit(solution)/shard_map/ppermute | solution.py:310
  171.7 2.4 %slice_add_fusion.1 = f32[1024,256]{1,0:T(8,128)} fusion(f32[2048,256]{1,0:T(8,128)} %copy-done, bf16[1024,256]{1,0:T(8,128)(2,1)} %collective-permute-done.10), kind=kLoop, calls=%fused_computation.5 | loop fusion | flops 524288 | bytes 2621440 | tf_op jit(solution)/shard_map/add | solution.py:360
  174.1 10.8 %collective-permute-done.8 = bf16[272,1024]{1,0:T(8,128)(2,1)S(1)} collective-permute-done((bf16[272,1024]{1,0:T(8,128)(2,1)S(1)}, bf16[272,1024]{1,0:T(8,128)(2,1)S(1)}, u32[]{:S(2)}, u32[]{:S(2)}) %collective-permute-start.8) | collective-permute-done | bytes 557088 | tf_op jit(solution)/shard_map/ppermute | solution.py:310
  185.1 1.0 slice.28
  186.8 2.6 %final.1 = (bf16[256,512]{1,0:T(8,128)(2,1)}, bf16[256,512]{1,0:T(8,128)(2,1)}) custom-call(s32[64]{0:T(128)} %get-tuple-element.25.slots, bf16[128,8,512]{2,1,0:T(8,128)(2,1)} %all-to-all-done.1.ret, f32[256,512]{1,0:T(8,128)} %get-tuple-element.30.base_o, f32[256,512]{1,0:T(8,128)} %get-tuple-element.31.base_k), custom_call_target="tpu_custom_call" | custom-call | flops 2000000000 | bytes 2000000 | tf_op jit(solution)/shard_map/final/pallas_call | solution.py:363
  189.4 2.0 %total.1 = f32[8,512]{1,0:T(8,128)} custom-call(bf16[128,8,512]{2,1,0:T(8,128)(2,1)} %all-to-all-done.3.recv), custom_call_target="tpu_custom_call" | custom-call | flops 1000000000 | bytes 1000000 | tf_op jit(solution)/shard_map/total/pallas_call | solution.py:366
  191.4 1.3 reshape.32
  (57 shorter events, 11.7 us)
Async XLA Ops:
  7.9 16.5 %copy-start.5 = (bf16[512,1024]{1,0:T(8,128)(2,1)S(1)}, bf16[512,1024]{1,0:T(8,128)(2,1)}, u32[]{:S(2)}) copy-start(bf16[512,1024]{1,0:T(8,128)(2,1)} %wi.1) | copy-start | bytes 3145732
  7.9 17.2 %copy-start.6 = (bf16[1024,512]{1,0:T(8,128)(2,1)S(1)}, bf16[1024,512]{1,0:T(8,128)(2,1)}, u32[]{:S(2)}) copy-start(bf16[1024,512]{1,0:T(8,128)(2,1)} %wo.1) | copy-start | bytes 3145732
  7.9 55.9 %all-to-all-start = ((bf16[128,8,640]{2,1,0:T(8,128)(2,1)}), bf16[128,8,640]{2,1,0:T(8,128)(2,1)S(1)}, u32[]{:S(2)}, u32[]{:S(2)}) async-start(bf16[128,8,640]{2,1,0:T(8,128)(2,1)} %get-tuple-element.26), calls=%async_computation | async-start | bytes 2621440 | tf_op jit(solution)/shard_map/all_to_all | solution.py:316
  24.5 23.2 %collective-permute-start = (bf16[256,1024]{1,0:T(8,128)(2,1)S(1)}, bf16[256,1024]{1,0:T(8,128)(2,1)S(1)}, u32[]{:S(2)}, u32[]{:S(2)}) collective-permute-start(bf16[256,1024]{1,0:T(8,128)(2,1)S(1)} %constant_dynamic-slice_fusion.2), channel_id=1, source_target_pairs={{0,2},{2,0},{4,6},{6,4},{8,10},{10,8},{12,14},{14,12},{16,18},{18,... | collective-permute-start | bytes 1572872 | tf_op jit(solution)/shard_map/ppermute | solution.py:310
  25.2 41.9 %copy-start.12 = (f32[1024]{0:T(1024)S(1)}, f32[1024]{0:T(1024)}, u32[]{:S(2)}) copy-start(f32[1024]{0:T(1024)} %param.13) | copy-start | bytes 12292
  25.2 37.8 %collective-permute-start.2 = (bf16[1024,256]{1,0:T(8,128)(2,1)S(1)}, bf16[1024,256]{1,0:T(8,128)(2,1)S(1)}, u32[]{:S(2)}, u32[]{:S(2)}) collective-permute-start(bf16[1024,256]{1,0:T(8,128)(2,1)S(1)} %constant_dynamic-slice_fusion.1), channel_id=1, source_target_pairs={{0,2},{2,0},{4,6},{6,4},{8,10},{10,8},{12,14},{14,12},{16,18},{18,... | collective-permute-start | bytes 1572872 | tf_op jit(solution)/shard_map/ppermute | solution.py:310
  47.7 35.2 %copy-start.8 = (bf16[256,1024]{1,0:T(8,128)(2,1)}, bf16[256,1024]{1,0:T(8,128)(2,1)S(1)}, u32[]{:S(2)}) copy-start(bf16[256,1024]{1,0:T(8,128)(2,1)S(1)} %collective-permute-done.wiy) | copy-start | bytes 1572868
  47.7 35.2 %collective-permute-start.1 = (bf16[256,1024]{1,0:T(8,128)(2,1)S(1)}, bf16[256,1024]{1,0:T(8,128)(2,1)S(1)}, u32[]{:S(2)}, u32[]{:S(2)}) collective-permute-start(bf16[256,1024]{1,0:T(8,128)(2,1)S(1)} %collective-permute-done.wiy), channel_id=1, source_target_pairs={{0,1},{1,0},{2,3},{3,2},{4,5},{5,4},{6,7},{7,6},{8,9},{9,8},{10,11... | collective-permute-start | bytes 1572872 | tf_op jit(solution)/shard_map/ppermute | solution.py:313
  63.0 20.0 %copy-start.9 = (bf16[1024,256]{1,0:T(8,128)(2,1)}, bf16[1024,256]{1,0:T(8,128)(2,1)S(1)}, u32[]{:S(2)}) copy-start(bf16[1024,256]{1,0:T(8,128)(2,1)S(1)} %collective-permute-done.2.woy) | copy-start | bytes 1572868
  63.0 19.9 %collective-permute-start.3 = (bf16[1024,256]{1,0:T(8,128)(2,1)S(1)}, bf16[1024,256]{1,0:T(8,128)(2,1)S(1)}, u32[]{:S(2)}, u32[]{:S(2)}) collective-permute-start(bf16[1024,256]{1,0:T(8,128)(2,1)S(1)} %collective-permute-done.2.woy), channel_id=1, source_target_pairs={{0,1},{1,0},{2,3},{3,2},{4,5},{5,4},{6,7},{7,6},{8,9},{9,8},{10,11... | collective-permute-start | bytes 1572872 | tf_op jit(solution)/shard_map/ppermute | solution.py:313
  67.0 1.4 collective-permute-start.5
  67.0 15.8 %collective-permute-start.4 = (f32[1024]{0:T(1024)S(1)}, f32[1024]{0:T(1024)S(1)}, u32[]{:S(2)}, u32[]{:S(2)}) collective-permute-start(f32[1024]{0:T(1024)S(1)} %copy-done.12), channel_id=1, source_target_pairs={{0,2},{2,0},{4,6},{6,4},{8,10},{10,8},{12,14},{14,12},{16,18},{18,... | collective-permute-start | bytes 12296 | tf_op jit(solution)/shard_map/ppermute | solution.py:310
  70.4 27.5 %all-to-all-start.2 = ((bf16[128,8,128]{2,1,0:T(8,128)(2,1)}), bf16[128,8,128]{2,1,0:T(8,128)(2,1)S(1)}, u32[]{:S(2)}, u32[]{:S(2)}) async-start(bf16[128,8,128]{2,1,0:T(8,128)(2,1)} %spread.1), calls=%async_computation.2 | async-start | bytes 524288 | tf_op jit(solution)/shard_map/all_to_all | solution.py:316
  97.8 13.6 %copy-start.4 = (bf16[128,8,128]{2,1,0:T(8,128)(2,1)}, bf16[128,8,128]{2,1,0:T(8,128)(2,1)S(1)}, u32[]{:S(2)}) copy-start(bf16[128,8,128]{2,1,0:T(8,128)(2,1)S(1)} %all-to-all-done.2.rs) | copy-start | bytes 786436
  97.8 41.8 %all-to-all-start.1 = ((bf16[128,8,512]{2,1,0:T(8,128)(2,1)}), bf16[128,8,512]{2,1,0:T(8,128)(2,1)}, u32[]{:S(2)}, u32[]{:S(2)}) async-start(bf16[128,8,512]{2,1,0:T(8,128)(2,1)} %get-tuple-element.27), calls=%async_computation.1 | async-start | bytes 2097152 | tf_op jit(solution)/shard_map/all_to_all | solution.py:316
  119.4 9.4 %collective-permute-start.6 = (bf16[256,2048]{1,0:T(8,128)(2,1)}, bf16[256,2048]{1,0:T(8,128)(2,1)S(1)}, u32[]{:S(2)}, u32[]{:S(2)}) collective-permute-start(bf16[256,2048]{1,0:T(8,128)(2,1)} %get-tuple-element.35), channel_id=1, source_target_pairs={{0,1},{1,0},{2,3},{3,2},{4,5},{5,4},{6,7},{7,6},{8,9},{9,8},{10,11... | collective-permute-start | bytes 3145736 | tf_op jit(solution)/shard_map/ppermute | solution.py:313
  128.4 19.9 %collective-permute-start.9 = (bf16[2048,256]{1,0:T(8,128)(2,1)}, bf16[2048,256]{1,0:T(8,128)(2,1)}, u32[]{:S(2)}, u32[]{:S(2)}) collective-permute-start(bf16[2048,256]{1,0:T(8,128)(2,1)} %get-tuple-element.43), channel_id=1, source_target_pairs={{0,1},{1,0},{2,3},{3,2},{4,5},{5,4},{6,7},{7,6},{8,9},{9,8},{10,11... | collective-permute-start | bytes 3145736 | tf_op jit(solution)/shard_map/ppermute | solution.py:313
  128.4 22.9 %collective-permute-start.7 = (bf16[272,2048]{1,0:T(8,128)(2,1)}, bf16[272,2048]{1,0:T(8,128)(2,1)S(1)}, u32[]{:S(2)}, u32[]{:S(2)}) collective-permute-start(bf16[272,2048]{1,0:T(8,128)(2,1)} %get-tuple-element.41), channel_id=1, source_target_pairs={{0,1},{1,0},{2,3},{3,2},{4,5},{5,4},{6,7},{7,6},{8,9},{9,8},{10,11... | collective-permute-start | bytes 3342344 | tf_op jit(solution)/shard_map/ppermute | solution.py:313
  134.0 14.3 %copy-start.2 = (f32[2048,256]{1,0:T(8,128)S(1)}, f32[2048,256]{1,0:T(8,128)}, u32[]{:S(2)}) copy-start(f32[2048,256]{1,0:T(8,128)} %get-tuple-element.42) | copy-start | bytes 6291460
  139.7 49.7 %all-to-all-start.3 = ((bf16[128,8,512]{2,1,0:T(8,128)(2,1)}), bf16[128,8,512]{2,1,0:T(8,128)(2,1)}, u32[]{:S(2)}, u32[]{:S(2)}) async-start(bf16[128,8,512]{2,1,0:T(8,128)(2,1)} %bitcast.5), calls=%async_computation.3 | async-start | bytes 2097152 | tf_op jit(solution)/shard_map/all_to_all | solution.py:316
  148.2 3.1 %copy-start.1 = (f32[272,2048]{1,0:T(8,128)S(1)}, f32[272,2048]{1,0:T(8,128)}, u32[]{:S(2)}) copy-start(f32[272,2048]{1,0:T(8,128)} %get-tuple-element.40) | copy-start | bytes 6684676
  149.8 1.5 copy-start
  150.8 20.9 %collective-permute-start.10 = (bf16[1024,256]{1,0:T(8,128)(2,1)}, bf16[1024,256]{1,0:T(8,128)(2,1)}, u32[]{:S(2)}, u32[]{:S(2)}) collective-permute-start(bf16[1024,256]{1,0:T(8,128)(2,1)} %slice.37), channel_id=1, source_target_pairs={{0,2},{2,0},{4,6},{6,4},{8,10},{10,8},{12,14},{14,12},{16,18},{18,... | collective-permute-start | bytes 1572872 | tf_op jit(solution)/shard_map/ppermute | solution.py:310
  151.7 33.2 %collective-permute-start.8 = (bf16[272,1024]{1,0:T(8,128)(2,1)S(1)}, bf16[272,1024]{1,0:T(8,128)(2,1)S(1)}, u32[]{:S(2)}, u32[]{:S(2)}) collective-permute-start(bf16[272,1024]{1,0:T(8,128)(2,1)S(1)} %slice.36), channel_id=1, source_target_pairs={{0,2},{2,0},{4,6},{6,4},{8,10},{10,8},{12,14},{14,12},{16,18},{18,... | collective-permute-start | bytes 1671176 | tf_op jit(solution)/shard_map/ppermute | solution.py:310
  (6 other events, 5.0 us)
